TPU v7x, 512 devices: a whole 4x4x16 slice. The times are simulated.
512 devices in a mesh: grp: 128 (over x, z, core), lev: 4 (over y).
Axes of the slice: x: 4, y: 4, z: 16, core: 2. Of those that a mesh axis runs over, the one named last changes fastest.
Arguments:
- spectrum: float32 [16, 640, 2, 640], P('lev', 'grp'), may hold values from -6 to 6
- wave_slot: int32 [640], replicated, may hold values from 0 to 639, each once
Outputs:
- new_spectrum: float32 [16, 640, 2, 640], P('lev', 'grp')
- products: float32 [16, 1024, 1440], P('lev', 'grp')
Inputs may be any that keep to these rules, and one draw needn't show every extreme that they name: Row s of the spectral arrays holds zonal wavenumber wave_slot[s]; every wavenumber below 640 appears exactly once.
All inputs are finite; a program needn't handle non-finite values.
Results may differ from a plain program's by a relative error of at most 0.0003.
Values sent between devices are 32-bit elements; how exact they have to be, the bound alone decides.
A program may use at most 128 MiB of HBM per device.

v0:
```python
import math

import jax
import jax.numpy as jnp
from jax import lax
from jax.sharding import PartitionSpec as P

NLON = 1440
LAT_DEV = 8


def swapped(value, axis, stride):
    return lax.ppermute(value, axis, [(i, i ^ 1 << stride) for i in range(lax.axis_size(axis))])


def parity_tables(lat_count, degrees):
    rows = jnp.arange(lat_count, dtype=jnp.int32)
    orders = jnp.arange(degrees, dtype=jnp.int32)
    odd_rows = 2 * rows[:, None] + 1
    even_steps = orders[None, :] * odd_rows % (4 * lat_count)
    odd_steps = ((orders[None, :] + 1) * odd_rows - lat_count) % (4 * lat_count)
    steps_both = jnp.stack([even_steps, odd_steps])
    return jnp.cos(steps_both.astype(jnp.float32) * (math.pi / (2 * lat_count)))


def lon_tables(wavenumbers, lon_count):
    cols = jnp.arange(lon_count, dtype=jnp.int32)
    phase_steps = wavenumbers[:, None] * cols[None, :] % lon_count
    angles = phase_steps.astype(jnp.float32) * (2.0 * math.pi / lon_count)
    return jnp.stack([jnp.cos(angles), -jnp.sin(angles)])


def wave_weight(wavenumbers):
    return jnp.where(wavenumbers == 0, 1.0, 2.0).astype(jnp.float32)


def longitude_synth(fourier, weights, tables):
    weighted = fourier * weights[None, None, :, None]
    return jnp.einsum("lcsj,csi->lji", weighted, tables, precision=lax.Precision.HIGHEST)


def longitude_analysis(paired, tables):
    return jnp.einsum("lji,csi->lcsj", paired, tables, precision=lax.Precision.HIGHEST) / NLON


def meridional_synth(spectrum, tables, odd_slots, kept):
    degrees = spectrum.shape[3]
    masked = jnp.where(kept[None, :, None, :], spectrum, jnp.zeros_like(spectrum))
    both = jnp.einsum("lscn,pjn->plcsj", masked, tables, precision=lax.Precision.HIGHEST) / degrees
    return jnp.where(odd_slots[None, None, :, None], both[1], both[0])


def meridional_analysis(fourier_back, tables, odd_slots, kept):
    lat_count = fourier_back.shape[3]
    degrees = tables.shape[2]
    both = jnp.einsum("lcsj,pjn->plscn", fourier_back, tables, precision=lax.Precision.HIGHEST) * (
        2.0 * degrees / lat_count
    )
    chosen = jnp.where(odd_slots[None, :, None, None], both[1], both[0])
    return jnp.where(kept[None, :, None, :], chosen, jnp.zeros_like(chosen))


def on_device(spectrum, wave_slot):
    degrees = spectrum.shape[3]
    slots_here = spectrum.shape[1]
    lat_count = LAT_DEV * lax.axis_size("grp")
    first_slot = lax.axis_index("grp") * slots_here
    local_waves = lax.dynamic_slice_in_dim(wave_slot, first_slot, slots_here)
    odd_slots = local_waves % 2 == 1
    kept = jnp.arange(degrees, dtype=jnp.int32)[None, :] >= local_waves[:, None]
    basis = parity_tables(lat_count, degrees)
    tables = lon_tables(wave_slot, NLON)
    weights = wave_weight(wave_slot)
    fourier = meridional_synth(spectrum, basis, odd_slots, kept)

    def to_grid(received):
        return longitude_synth(received, weights, tables)

    grid_values = to_grid(lax.all_to_all(fourier, "grp", split_axis=3, concat_axis=2, tiled=True))
    pair_bit = lax.axis_size("lev").bit_length() - 2
    partner = swapped(grid_values, "lev", pair_bit)
    paired = grid_values * partner + grid_values
    fourier_back = longitude_analysis(paired, tables)
    new_spectrum = meridional_analysis(
        lax.all_to_all(fourier_back, "grp", split_axis=2, concat_axis=3, tiled=True),
        basis,
        odd_slots,
        kept,
    )
    fourier_new = meridional_synth(new_spectrum, basis, odd_slots, kept)
    products = to_grid(lax.all_to_all(fourier_new, "grp", split_axis=3, concat_axis=2, tiled=True))
    return (new_spectrum, products)


def solution(mesh):
    return jax.shard_map(
        on_device,
        mesh=mesh,
        in_specs=(P("lev", "grp", None, None), P()),
        out_specs=(P("lev", "grp", None, None), P("lev", "grp", None)),
        check_vma=False,
    )
```

profile of v0, /device:TPU:1, one launch (start us, length us, event | category | flops | bytes accessed | tf_op | source)
XLA Modules:
  0.0 280.0 jit_solution(6767642680163371989)
XLA Ops:
  5.3 21.9 %fusion.38 = f32[2,4,2,5,1024]{4,3,2,1,0:T(8,128)S(1)} fusion(s32[1,1024,640]{2,1,0:T(8,128)S(1)} %get-tuple-element.13, s32[1,1024,640]{2,1,0:T(8,128)S(1)} %get-tuple-element.12, f32[4,5,2,640]{3,2,1,0:T(2,128)S(1)} %copy-done.7, pred[5,640]{1,0:T(8,128)(4,1)S(1)} %iota_compare_fusion), kind=kOutput, calls=%fused_computation.43 | convolution fusion | flops 633185280 | bytes 5676160 | tf_op jit(solution)/shard_map/lscn,pjn->plcsj/dot_general | solution.py:49
  27.3 4.4 %copy.19 = f32[4,2,5,1024]{2,1,0,3:T(2,128)} copy(f32[4,2,5,1024]{3,2,1,0:T(8,128)S(1)} %fusion.60) | data formatting | bytes 327680 | tf_op jit(solution)/shard_map/jit(_where)/select_n | solution.py:50
  31.7 7.5 %reshape.267 = f32[128,1,320]{2,1,0:T(1,128)} reshape(f32[1024,4,2,5]{3,2,1,0:T(2,128)} %bitcast.121) | data formatting | bytes 327680
  39.2 20.4 %all-to-all-start = ((f32[128,1,320]{2,1,0:T(1,128)}), f32[128,1,320]{2,1,0:T(1,128)S(1)}, u32[]{:S(2)}, u32[]{:S(2)}) async-start(f32[128,1,320]{2,1,0:T(1,128)} %reshape.267), calls=%async_computation | async-start | bytes 393216 | tf_op jit(solution)/shard_map/all_to_all | solution.py:79
  59.6 17.0 %fusion.13 = (f32[1,640,1440]{1,2,0:T(8,128)}, f32[1,640,1440]{1,2,0:T(8,128)}) fusion(s32[640]{0:T(1024)S(1)} %copy-done.6), kind=kLoop, calls=%fused_computation.26 | loop fusion | flops 9216000 | bytes 7375360 | tf_op jit(solution)/shard_map/cos | solution.py:30
  76.6 3.0 %all-to-all-done = f32[128,1,320]{2,1,0:T(1,128)S(1)} async-done(((f32[128,1,320]{2,1,0:T(1,128)}), f32[128,1,320]{2,1,0:T(1,128)S(1)}, u32[]{:S(2)}, u32[]{:S(2)}) %all-to-all-start) | async-done | bytes 163872 | tf_op jit(solution)/shard_map/all_to_all | solution.py:79
  81.3 7.5 %reshape.268 = f32[1024,4,2,5]{3,2,1,0:T(2,128)} reshape(f32[128,320]{1,0:T(8,128)S(1)} %reduce) | data formatting | bytes 327680
  88.8 6.6 %copy.52 = f32[4,2,5,128,8]{2,3,4,1,0:T(8,128)} copy(f32[4,2,5,128,8]{2,1,0,4,3:T(2,128)} %bitcast.122) | data formatting | bytes 327680 | tf_op jit(solution)/shard_map/all_to_all | solution.py:79
  95.4 3.3 %all_to_all.42 = f32[4,2,640,8]{2,3,1,0:T(8,128)S(1)} reshape(f32[4,2,128,5,8]{3,2,4,1,0:T(8,128)} %bitcast.123) | data formatting | bytes 327680 | tf_op jit(solution)/shard_map/all_to_all | solution.py:79
  98.8 10.0 %fusion.29 = f32[4,8,1440]{2,1,0:T(8,128)S(1)} fusion(f32[1,640,1440]{1,2,0:T(8,128)} %get-tuple-element.11, f32[1,640,1440]{1,2,0:T(8,128)} %get-tuple-element.10, f32[4,2,640,8]{2,3,1,0:T(8,128)S(1)} %all_to_all.42, f32[640]{0:T(1024)S(1)} %compare_select_fusion), kind=kOutput, calls=%fused_computation.40 | convolution fusion | flops 709672960 | bytes 7723520 | tf_op jit(solution)/shard_map/lcsj,csi->lji/dot_general | solution.py:39
  108.8 5.2 %collective-permute-start = (f32[4,8,1440]{2,1,0:T(8,128)S(1)}, f32[4,8,1440]{2,1,0:T(8,128)S(1)}, u32[]{:S(2)}, u32[]{:S(2)}) collective-permute-start(f32[4,8,1440]{2,1,0:T(8,128)S(1)} %fusion.29), channel_id=1, source_target_pairs={{0,2},{1,3},{2,0},{3,1},{4,6},{5,7},{6,4},{7,5},{8,10},{9,11},{10,... | collective-permute-start | bytes 552968 | tf_op jit(solution)/shard_map/ppermute | solution.py:13
  116.7 4.1 %fusion.56 = f32[4,2,640,8]{2,3,0,1:T(8,128)S(1)} fusion(f32[1,640,1440]{1,2,0:T(8,128)S(1)} %copy-done.1, f32[1,640,1440]{1,2,0:T(8,128)S(1)} %copy-done, f32[4,8,1440]{2,1,0:T(8,128)S(1)} %fusion.29, f32[4,8,1440]{2,1,0:T(8,128)S(1)} %collective-permute-done), kind=kOutput, calls=%fused_computation.49 | convolution fusion | flops 709765120 | bytes 7905280 | tf_op jit(solution)/shard_map/lji,csi->lcsj/dot_general | solution.py:43
  124.0 36.0 %all_to_all.54 = f32[128,1,320]{2,1,0:T(1,128)S(1)} all-to-all(f32[128,1,320]{2,1,0:T(1,128)S(1)} %reshape.269), channel_id=1, replica_groups=mesh['grp'=128,'lev'=4] {'grp'}, dimensions={0} | all-to-all | bytes 327680 | tf_op jit(solution)/shard_map/all_to_all | solution.py:85
  165.0 2.9 %all_to_all.46 = f32[4,2,5,1024]{3,1,2,0:T(2,128)S(1)} reshape(f32[4,2,5,128,8]{4,3,1,2,0:T(8,128)} %bitcast.129) | data formatting | bytes 327680 | tf_op jit(solution)/shard_map/all_to_all | solution.py:85
  167.9 22.0 %fusion.50 = f32[2,4,5,2,640]{4,2,3,1,0:T(8,128)S(1)} fusion(s32[1,1024,640]{2,1,0:T(8,128)} %copy-done.4, s32[1,1024,640]{2,1,0:T(8,128)} %copy-done.2, f32[4,2,5,1024]{3,1,2,0:T(2,128)S(1)} %all_to_all.46), kind=kOutput, calls=%fused_computation.47 | convolution fusion | flops 633128960 | bytes 5611520 | tf_op jit(solution)/shard_map/lcsj,pjn->plscn/dot_general | solution.py:56
  190.1 22.0 %fusion.44 = f32[2,4,2,5,1024]{4,3,2,1,0:T(8,128)S(1)} fusion(s32[1,1024,640]{2,1,0:T(8,128)S(1)} %copy-done.5, s32[1,1024,640]{2,1,0:T(8,128)S(1)} %copy-done.3, f32[4,5,2,640]{3,1,2,0:T(8,128)S(1)} %fusion.66, pred[5,640]{1,0:T(8,128)(4,1)S(1)} %iota_compare_fusion), kind=kOutput, calls=%fused_computation.45 | convolution fusion | flops 633185280 | bytes 5676160 | tf_op jit(solution)/shard_map/lscn,pjn->plcsj/dot_general | solution.py:49
  212.2 4.4 %copy.26 = f32[4,2,5,1024]{2,1,0,3:T(2,128)} copy(f32[4,2,5,1024]{3,2,1,0:T(8,128)S(1)} %fusion.59) | data formatting | bytes 327680 | tf_op jit(solution)/shard_map/jit(_where)/select_n | solution.py:50
  216.6 7.5 %reshape.271 = f32[128,1,320]{2,1,0:T(1,128)} reshape(f32[1024,4,2,5]{3,2,1,0:T(2,128)} %bitcast.124) | data formatting | bytes 327680
  224.1 6.6 %all-to-all-start.2 = ((f32[128,1,320]{2,1,0:T(1,128)}), f32[128,1,320]{2,1,0:T(1,128)S(1)}, u32[]{:S(2)}, u32[]{:S(2)}) async-start(f32[128,1,320]{2,1,0:T(1,128)} %reshape.271), calls=%async_computation.2 | async-start | bytes 393216 | tf_op jit(solution)/shard_map/all_to_all | solution.py:91
  231.5 19.4 %all-to-all-done.2 = f32[128,1,320]{2,1,0:T(1,128)S(1)} async-done(((f32[128,1,320]{2,1,0:T(1,128)}), f32[128,1,320]{2,1,0:T(1,128)S(1)}, u32[]{:S(2)}, u32[]{:S(2)}) %all-to-all-start.2) | async-done | bytes 163872 | tf_op jit(solution)/shard_map/all_to_all | solution.py:91
  252.0 7.5 %reshape.272 = f32[1024,4,2,5]{3,2,1,0:T(2,128)} reshape(f32[128,320]{1,0:T(8,128)S(1)} %reduce.2) | data formatting | bytes 327680
  259.5 6.6 %copy.51 = f32[4,2,5,128,8]{2,3,4,1,0:T(8,128)} copy(f32[4,2,5,128,8]{2,1,0,4,3:T(2,128)} %bitcast.125) | data formatting | bytes 327680 | tf_op jit(solution)/shard_map/all_to_all | solution.py:91
  266.1 3.3 %all_to_all.50 = f32[4,2,640,8]{2,3,1,0:T(8,128)S(1)} reshape(f32[4,2,128,5,8]{3,2,4,1,0:T(8,128)} %bitcast.126) | data formatting | bytes 327680 | tf_op jit(solution)/shard_map/all_to_all | solution.py:91
  269.5 10.1 %fusion.32 = f32[4,8,1440]{2,1,0:T(8,128)} fusion(f32[1,640,1440]{1,2,0:T(8,128)} %get-tuple-element.11, f32[1,640,1440]{1,2,0:T(8,128)} %get-tuple-element.10, f32[4,2,640,8]{2,3,1,0:T(8,128)S(1)} %all_to_all.50, f32[640]{0:T(1024)S(1)} %compare_select_fusion), kind=kOutput, calls=%fused_computation.41 | convolution fusion | flops 709672960 | bytes 7723520 | tf_op jit(solution)/shard_map/lcsj,csi->lji/dot_general | solution.py:39
  (35 shorter events, 19.3 us)
Async XLA Ops:
  0.6 4.7 %copy-start.7 = (f32[4,5,2,640]{3,2,1,0:T(2,128)S(1)}, f32[4,5,2,640]{3,2,1,0:T(2,128)}, u32[]{:S(2)}) copy-start(f32[4,5,2,640]{3,2,1,0:T(2,128)} %param.2) | copy-start | bytes 307204
  3.8 1.5 copy-start.2
  3.8 23.4 %copy-start.4 = (s32[1,1024,640]{2,1,0:T(8,128)}, s32[1,1024,640]{2,1,0:T(8,128)S(1)}, u32[]{:S(2)}) copy-start(s32[1,1024,640]{2,1,0:T(8,128)S(1)} %get-tuple-element.13) | copy-start | bytes 7864324
  27.3 32.3 %copy-start.6 = (s32[640]{0:T(1024)S(1)}, s32[640]{0:T(1024)}, u32[]{:S(2)}) copy-start(s32[640]{0:T(1024)} %param.3) | copy-start | bytes 7684
  39.2 40.4 %all-to-all-start = ((f32[128,1,320]{2,1,0:T(1,128)}), f32[128,1,320]{2,1,0:T(1,128)S(1)}, u32[]{:S(2)}, u32[]{:S(2)}) async-start(f32[128,1,320]{2,1,0:T(1,128)} %reshape.267), calls=%async_computation | async-start | bytes 393216 | tf_op jit(solution)/shard_map/all_to_all | solution.py:79
  98.8 17.9 %copy-start = (f32[1,640,1440]{1,2,0:T(8,128)S(1)}, f32[1,640,1440]{1,2,0:T(8,128)}, u32[]{:S(2)}) copy-start(f32[1,640,1440]{1,2,0:T(8,128)} %get-tuple-element.10) | copy-start | bytes 11059204
  98.8 17.9 %copy-start.1 = (f32[1,640,1440]{1,2,0:T(8,128)S(1)}, f32[1,640,1440]{1,2,0:T(8,128)}, u32[]{:S(2)}) copy-start(f32[1,640,1440]{1,2,0:T(8,128)} %get-tuple-element.11) | copy-start | bytes 11059204
  108.8 7.9 %collective-permute-start = (f32[4,8,1440]{2,1,0:T(8,128)S(1)}, f32[4,8,1440]{2,1,0:T(8,128)S(1)}, u32[]{:S(2)}, u32[]{:S(2)}) collective-permute-start(f32[4,8,1440]{2,1,0:T(8,128)S(1)} %fusion.29), channel_id=1, source_target_pairs={{0,2},{1,3},{2,0},{3,1},{4,6},{5,7},{6,4},{7,5},{8,10},{9,11},{10,... | collective-permute-start | bytes 552968 | tf_op jit(solution)/shard_map/ppermute | solution.py:13
  167.9 22.2 %copy-start.3 = (s32[1,1024,640]{2,1,0:T(8,128)S(1)}, s32[1,1024,640]{2,1,0:T(8,128)}, u32[]{:S(2)}) copy-start(s32[1,1024,640]{2,1,0:T(8,128)} %copy-done.2) | copy-start | bytes 7864324
  167.9 22.2 %copy-start.5 = (s32[1,1024,640]{2,1,0:T(8,128)S(1)}, s32[1,1024,640]{2,1,0:T(8,128)}, u32[]{:S(2)}) copy-start(s32[1,1024,640]{2,1,0:T(8,128)} %copy-done.4) | copy-start | bytes 7864324
  224.1 26.7 %all-to-all-start.2 = ((f32[128,1,320]{2,1,0:T(1,128)}), f32[128,1,320]{2,1,0:T(1,128)S(1)}, u32[]{:S(2)}, u32[]{:S(2)}) async-start(f32[128,1,320]{2,1,0:T(1,128)} %reshape.271), calls=%async_computation.2 | async-start | bytes 393216 | tf_op jit(solution)/shard_map/all_to_all | solution.py:91
where the time goes:
time: 283 us; the launch traced here: 280 us
  matrix products  90.1 us (32%)
  local copies, waits for them, and re-layouts  71.4 us (25%)
  blocking collectives  36 us (13%)
  starting transfers between devices  32.3 us (11%)
  waiting for transfers between devices  25 us (9%)
  other arithmetic  23.8 us (8%)
    dot_general x2, matrix products, meridional_synth(): jnp.einsum('lscn,pjn->plcsj', masked, tables, precision=lax.Precision.HIG...  43.9 us
    unnamed x23, local copies, waits for them, and re-layouts  36.1 us
    all_to_all x1, blocking collectives, on_device(): lax.all_to_all(fourier_back, 'grp', split_axis=2, concat_axis=3, tiled=True)  36 us
    dot_general x1, matrix products, meridional_analysis(): jnp.einsum('lcsj,pjn->plscn', fourier_back, tables, precision=lax.Precisi...  22 us
    all_to_all x1, starting transfers between devices, on_device(): lax.all_to_all(fourier, 'grp', split_axis=3, concat_axis=2, tiled=True)  20.4 us
    dot_general x2, matrix products, longitude_synth(): jnp.einsum('lcsj,csi->lji', weighted, tables, precision=lax.Precision.HIG...  20.1 us
    all_to_all x1, waiting for transfers between devices, on_device(): lax.all_to_all(fourier_new, 'grp', split_axis=3, concat_axis=2, tiled=True)  19.4 us
    cos x1, other arithmetic, lon_tables(): return jnp.stack([jnp.cos(angles), -jnp.sin(angles)])  17 us
  transfers between devices with their start and end apart: 3, of which 3 were waited for; matrix products, arithmetic and copies ran while one was open for 6% of the time, Pallas kernels for 0%

commit v1 on v0

v1 whole, which is shorter than its diff:
```python
import functools
import math

import jax
import jax.numpy as jnp
import numpy as np
from jax import lax
from jax.experimental import pallas as pl
from jax.experimental.pallas import tpu as pltpu
from jax.sharding import PartitionSpec as P

NLON = 1440
LANES = 1536
NN = 640
NLAT = 1024
CHIPS = 64
SLOTS = 10
MESH = pl.DeviceIdType.MESH
F32 = jnp.float32
BF16 = jnp.bfloat16


def meridional_parts():
    chips = np.arange(CHIPS)
    coarse, fine = [], []
    odd_rows = 16 * np.arange(2)[:, None] + 2 * np.arange(8)[None, :] + 1
    for shift in range(2):
        k = np.arange(NN) + shift
        a = 2.0 * np.pi * ((chips[:, None] * k[None, :]) % 128) / 128.0
        b = np.pi * ((odd_rows[:, :, None] * k) % 4096) / 2048.0
        coarse += [np.cos(a), np.sin(a)]
        fine += [np.cos(b), np.sin(b)]
    return np.stack(coarse).astype(np.float32), np.stack(fine, axis=2).astype(np.float32)


def split(value):
    high = value.astype(BF16)
    return high, (value - high.astype(F32)).astype(BF16)


def dot_nn(a, b):
    return lax.dot_general(a, b, (((1,), (0,)), ((), ())), preferred_element_type=F32)


def dot_nt(a, b):
    return lax.dot_general(a, b, (((1,), (1,)), ((), ())), preferred_element_type=F32)


def cos_sin(steps):
    turn = steps - 1440.0 * jnp.floor((steps + 0.5) * (1.0 / 1440.0))
    quarter = jnp.floor((turn + 180.0) * (1.0 / 360.0) + 1e-4)
    t = (turn - 360.0 * quarter) * (2.0 * math.pi / 1440.0)
    u = t * t
    s = t * (1.0 + u * (-1.0 / 6 + u * (1.0 / 120 + u * (-1.0 / 5040 + u * (1.0 / 362880)))))
    c = 1.0 + u * (-0.5 + u * (1.0 / 24 + u * (-1.0 / 720 + u * (1.0 / 40320 + u * (-1.0 / 3628800)))))
    swap = (quarter == 1.0) | (quarter == 3.0)
    cos, sin = jnp.where(swap, s, c), jnp.where(swap, c, s)
    cos = jnp.where((quarter == 1.0) | (quarter == 2.0), -cos, cos)
    sin = jnp.where((quarter == 2.0) | (quarter == 3.0), -sin, sin)
    return cos, sin


def kernel(
    x_ref, waves_ref, wave_scalars, coarse_ref, fine_ref,
    new_ref, products_ref,
    spec, part, part_in, mer_hi, mer_lo, weights_x, lon_hi, lon_lo, weights_p,
    send1, recv1, send2, recv2, send3, recv3, grid, grid_in, final,
    pair_send, pair_recv, all_send, all_recv, lev_send, lev_recv,
):
    me, level = lax.axis_index("grp"), lax.axis_index("lev")
    core, chip = lax.rem(me, 2), me // 2
    sibling = {"grp": 2 * chip + 1 - core}
    partner = {"lev": lax.rem(level + 2, 4)}

    def peer(step):
        return lax.rem(chip + step, CHIPS)

    barrier = pltpu.get_barrier_semaphore()

    @pl.loop(1, CHIPS)
    def _(step):
        pl.semaphore_signal(barrier, inc=1, device_id={"grp": 2 * peer(step) + core}, device_id_type=MESH)

    pl.semaphore_signal(barrier, inc=1, device_id=sibling, device_id_type=MESH)
    pl.semaphore_signal(barrier, inc=1, device_id=partner, device_id_type=MESH)

    for s in range(5):
        for c in range(2):
            spec[5 * core + s, 4 * c:4 * c + 4, :] = x_ref[:, s, c, :]

    @pl.loop(0, 8)
    def _(row):
        fine = fine_ref[core, row]
        for parity in range(2):
            fc, fs = fine[2 * parity:2 * parity + 1], fine[2 * parity + 1:2 * parity + 2]
            for block in range(4):
                rows = slice(16 * block, 16 * block + 16)
                cc, cs = coarse_ref[2 * parity, rows, :], coarse_ref[2 * parity + 1, rows, :]
                value = cc * fc - cs * fs if parity == 0 else cs * fc + cc * fs
                high, low = split(value)
                where = pl.ds(pl.multiple_of(row * CHIPS + 16 * block, 16), 16)
                columns = slice(NN * parity, NN * parity + NN)
                mer_hi[where, columns] = high
                mer_lo[where, columns] = low

    lane = lax.broadcasted_iota(jnp.int32, (16, 128), 1)
    lane_f = lane.astype(F32)
    for s in range(SLOTS):
        @pl.loop(0, 4)
        def _(block):
            wave = waves_ref[pl.ds(pl.multiple_of(16 * block, 16), 16), s:s + 1] + jnp.zeros((16, 128), F32)
            cos, sin = cos_sin(wave * lane_f)
            turn_cos, turn_sin = cos_sin(wave * 128.0)
            first = pl.multiple_of(s * CHIPS + 16 * block, 16)
            second = pl.multiple_of((SLOTS + s) * CHIPS + 16 * block, 16)
            for a in range(LANES // 128):
                columns = slice(128 * a, 128 * a + 128)
                put_cos, put_sin = cos, -sin
                if 128 * a + 128 > NLON:
                    inside = lane < NLON - 128 * a
                    put_cos, put_sin = jnp.where(inside, put_cos, 0.0), jnp.where(inside, put_sin, 0.0)
                lon_hi[pl.ds(first, 16), columns], lon_lo[pl.ds(first, 16), columns] = split(put_cos)
                lon_hi[pl.ds(second, 16), columns], lon_lo[pl.ds(second, 16), columns] = split(put_sin)
                if 128 * a + 128 < LANES:
                    cos, sin = cos * turn_cos - sin * turn_sin, sin * turn_cos + cos * turn_sin

    weights_x[...] = jnp.zeros_like(weights_x)
    weights_p[...] = jnp.zeros_like(weights_p)

    pl.semaphore_wait(barrier, CHIPS + 1)

    def pair_copy(index, source, target):
        return pltpu.make_async_remote_copy(
            src_ref=source, dst_ref=target, send_sem=pair_send.at[index], recv_sem=pair_recv.at[index],
            device_id=sibling, device_id_type=MESH)

    mine = spec.at[pl.ds(5 * core, 5)]
    copy = pair_copy(0, mine, mine)
    copy.start()
    copy.wait()

    degree = lax.broadcasted_iota(jnp.int32, (8, NN), 1)
    lane64 = lax.broadcasted_iota(jnp.int32, (CHIPS, 128), 1)
    lane8 = lax.broadcasted_iota(jnp.int32, (8, 128), 1)
    sub8 = lax.broadcasted_iota(jnp.int32, (8, 128), 0)

    def slot_wave(s):
        return wave_scalars[SLOTS * chip + s]

    def exchange(index, out, inbox):
        @pl.loop(1, CHIPS)
        def _(step):
            to = peer(step)
            pltpu.make_async_remote_copy(
                src_ref=out.at[to], dst_ref=inbox.at[chip], send_sem=all_send.at[index], recv_sem=all_recv.at[index],
                device_id={"grp": 2 * to + core}, device_id_type=MESH).start()

        inbox[chip] = out[chip]
        arrived = inbox.at[pl.ds(0, CHIPS - 1)]
        pltpu.make_async_copy(arrived, arrived, all_recv.at[index]).wait()
        left = out.at[pl.ds(0, CHIPS - 1)]
        pltpu.make_async_copy(left, left, all_send.at[index]).wait()

    def meridional_synth(source, out):
        for parity in range(2):
            for half in range(5):
                rows = []
                for s in (2 * half, 2 * half + 1):
                    wave = slot_wave(s)
                    odd = wave % 2
                    chosen = odd if parity else 1 - odd
                    scale = chosen.astype(F32) * jnp.where(wave == 0, 1.0 / NN, 2.0 / NN)
                    rows.append(jnp.where(degree >= wave, source[s] * scale, 0.0))
                high, low = split(jnp.concatenate(rows, axis=0))
                columns = slice(NN * parity, NN * parity + NN)
                weights_x[16 * half:16 * half + 16, columns] = high
                weights_x[128 + 16 * half:128 + 16 * half + 16, columns] = low
        both = dot_nt(mer_hi[...], weights_x[...])
        value = both[:, :128] + both[:, 128:] + dot_nt(mer_lo[...], weights_x[:128, :])
        tiles = [None] * 5

        def put(t, piece):
            tiles[t] = piece if tiles[t] is None else tiles[t] + piece

        for row in range(8):
            t, offset = divmod(80 * row, 128)
            piece = value[CHIPS * row:CHIPS * row + CHIPS, :]
            if offset:
                piece = pltpu.roll(piece, offset, 1)
            if offset + 80 > 128:
                put(t, jnp.where(lane64 >= offset, piece, 0.0))
                put(t + 1, jnp.where(lane64 < offset, piece, 0.0))
            else:
                put(t, piece)
        for t in range(5):
            out[:, t, :] = tiles[t]

    def turned(inbox):
        result = []
        for t in range(5):
            block = inbox[:, t, :]
            result.append(jnp.concatenate([block, block], axis=0).T)
        return result

    def longitude_operand(inbox):
        tiles = turned(inbox)

        def group(row, s):
            t, offset = divmod(80 * row + 8 * s, 128)
            return tiles[t][offset:offset + 8, :]

        real, imag = [], []
        for pair in range(4):
            real_row, imag_row = [], []
            for half in range(5):
                a, b = (
                    jnp.where(lane8 < 64, group(row, 2 * half), group(row, 2 * half + 1))
                    for row in (2 * pair, 2 * pair + 1))
                real_row.append(jnp.where(sub8 < 4, a, pltpu.roll(b, 4, 0)))
                imag_row.append(jnp.where(sub8 < 4, pltpu.roll(a, 4, 0), b))
            real.append(jnp.concatenate(real_row, axis=1))
            imag.append(jnp.concatenate(imag_row, axis=1))
        value = jnp.concatenate([jnp.concatenate(real, axis=0), jnp.concatenate(imag, axis=0)], axis=1)
        return split(value)

    def longitude_synth(high, low, columns):
        both = dot_nn(jnp.concatenate([high, low], axis=0), lon_hi[:, columns])
        return both[:32] + both[32:] + dot_nn(high, lon_lo[:, columns])

    meridional_synth(spec, send1)
    exchange(0, send1, recv1)
    high, low = longitude_operand(recv1)
    copies = []
    for a in range(3):
        grid[a] = longitude_synth(high, low, slice(512 * a, 512 * a + 512))
        copy = pltpu.make_async_remote_copy(
            src_ref=grid.at[a], dst_ref=grid_in.at[a], send_sem=lev_send.at[a], recv_sem=lev_recv.at[a],
            device_id=partner, device_id_type=MESH)
        copy.start()
        copies.append(copy)
    for a in range(3):
        copies[a].wait()
        here = grid[a]
        high, low = split(here * grid_in[a] + here)
        weights_p[0:32, 512 * a:512 * a + 512] = high
        weights_p[128:160, 512 * a:512 * a + 512] = low

    both = dot_nt(lon_hi[...], weights_p[...])
    value = both[:, :128] + both[:, 128:] + dot_nt(lon_lo[...], weights_p[:128, :])
    for t in range(5):
        tile = None
        for s in range(2):
            for c in range(2):
                first = (c * SLOTS + 2 * t + s) * CHIPS
                piece = value[first:first + CHIPS, :]
                offset = 64 * s + 32 * c
                piece = pltpu.roll(piece, offset, 1) if offset else piece
                tile = piece if tile is None else tile + piece
        send2[:, t, :] = tile
    exchange(1, send2, recv2)

    tiles = turned(recv2)
    rows = []
    for s in range(SLOTS):
        row = []
        for pair in range(4):
            a, b = (
                tiles[s // 2][64 * (s % 2) + 32 * c + 8 * pair:64 * (s % 2) + 32 * c + 8 * pair + 8, :] for c in range(2))
            left = jnp.where(sub8 < 4, a, pltpu.roll(b, 4, 0))
            right = jnp.where(sub8 < 4, pltpu.roll(a, 4, 0), b)
            row.append(jnp.where(lane8 < 64, left, right))
        rows.append(jnp.concatenate(row, axis=1))
    high, low = split(jnp.concatenate(rows, axis=0))
    both = dot_nn(jnp.concatenate([high, low], axis=0), mer_hi[...])
    value = both[:80] + both[80:] + dot_nn(high, mer_lo[...])
    for s in range(SLOTS):
        wave = slot_wave(s)
        odd = (wave % 2).astype(F32)
        chosen = value[8 * s:8 * s + 8, :NN] * (1.0 - odd) + value[8 * s:8 * s + 8, NN:] * odd
        part[s] = jnp.where(degree >= wave, chosen * (2.0 * NN / NLAT / NLON), 0.0)
    copy = pair_copy(1, part, part_in)
    copy.start()
    copy.wait()
    for s in range(SLOTS):
        spec[s] = part[s] + part_in[s]
    for s in range(5):
        for c in range(2):
            new_ref[:, s, c, :] = spec[5 * core + s, 4 * c:4 * c + 4, :]

    meridional_synth(spec, send3)
    exchange(2, send3, recv3)
    high, low = longitude_operand(recv3)
    for a in range(3):
        value = longitude_synth(high, low, slice(512 * a, 512 * a + 512))
        for b in range(4):
            tile = 4 * a + b
            width = min(128, NLON - 128 * tile)
            final[tile] = value[:, 128 * b:128 * b + 128]
            for l in range(4):
                products_ref[l, :, 128 * tile:128 * tile + width] = final[tile, pl.ds(l, 8, stride=4), :][:, :width]


def on_device(spectrum, wave_slot):
    coarse, fine = meridional_parts()
    vmem, smem = pl.BlockSpec(memory_space=pltpu.VMEM), pl.BlockSpec(memory_space=pltpu.SMEM)
    message = pltpu.VMEM((CHIPS, 5, 128), F32)
    return pl.pallas_call(
        kernel,
        out_shape=(
            jax.ShapeDtypeStruct((4, 5, 2, NN), F32),
            jax.ShapeDtypeStruct((4, 8, NLON), F32),
        ),
        in_specs=[vmem, vmem, smem, vmem, vmem],
        out_specs=(vmem, vmem),
        scratch_shapes=[
            pltpu.VMEM((SLOTS, 8, NN), F32),
            pltpu.VMEM((SLOTS, 8, NN), F32),
            pltpu.VMEM((SLOTS, 8, NN), F32),
            pltpu.VMEM((8 * CHIPS, 2 * NN), BF16),
            pltpu.VMEM((8 * CHIPS, 2 * NN), BF16),
            pltpu.VMEM((256, 2 * NN), BF16),
            pltpu.VMEM((2 * SLOTS * CHIPS, LANES), BF16),
            pltpu.VMEM((2 * SLOTS * CHIPS, LANES), BF16),
            pltpu.VMEM((256, LANES), BF16),
            message, message, message, message, message, message,
            pltpu.VMEM((3, 32, 512), F32),
            pltpu.VMEM((3, 32, 512), F32),
            pltpu.VMEM((12, 32, 128), F32),
            pltpu.SemaphoreType.DMA((2,)),
            pltpu.SemaphoreType.DMA((2,)),
            pltpu.SemaphoreType.DMA((3,)),
            pltpu.SemaphoreType.DMA((3,)),
            pltpu.SemaphoreType.DMA((3,)),
            pltpu.SemaphoreType.DMA((3,)),
        ],
        compiler_params=pltpu.CompilerParams(collective_id=0, has_side_effects=True, vmem_limit_bytes=48 << 20),
    )(spectrum, wave_slot.reshape(CHIPS, SLOTS).astype(F32), wave_slot, jnp.asarray(coarse), jnp.asarray(fine))


def solution(mesh):
    return jax.shard_map(
        on_device,
        mesh=mesh,
        in_specs=(P("lev", "grp", None, None), P()),
        out_specs=(P("lev", "grp", None, None), P("lev", "grp", None)),
        check_vma=False,
    )
```

time: 283 us -> 83.4 us (0.29)
  matrix products: 90.1 us -> 0 us
  Pallas kernels: 0 us -> 76.8 us
  local copies, waits for them, and re-layouts: 71.4 us -> 4.9 us
  blocking collectives: 36 us -> 0 us
  starting transfers between devices: 32.3 us -> 0 us
  waiting for transfers between devices: 25 us -> 0 us
  other arithmetic: 23.8 us -> 0.69 us
    dot_general x6 -> x0, matrix products: 90.1 us -> none  [the longest x2 43.9 us: meridional_synth(): jnp.einsum('lscn,pjn->plcsj', masked, tables, precision=lax.Precision.HIG...]
    pallas_call x0 -> x1, Pallas kernels: none -> 76.8 us  [on_device(): pl.pallas_call(kernel, out_shape=(jax.ShapeDtypeStruct((4, 5, 2, NN), F32...]
    all_to_all x1 -> x0, blocking collectives: 36 us -> none  [on_device(): lax.all_to_all(fourier_back, 'grp', split_axis=2, concat_axis=3, tiled=True)]
    unnamed x23 -> x10, local copies, waits for them, and re-layouts: 36.1 us -> 4.77 us
    all_to_all x2 -> x0, starting transfers between devices: 27 us -> none  [the longest x1 20.4 us: on_device(): lax.all_to_all(fourier, 'grp', split_axis=3, concat_axis=2, tiled=True)]
    all_to_all x7 -> x0, local copies, waits for them, and re-layouts: 25.3 us -> none  [the longest x3 10.5 us: on_device(): lax.all_to_all(fourier, 'grp', split_axis=3, concat_axis=2, tiled=True)]
    all_to_all x2 -> x0, waiting for transfers between devices: 22.3 us -> none  [the longest x1 19.4 us: on_device(): lax.all_to_all(fourier_new, 'grp', split_axis=3, concat_axis=2, tiled=True)]
    cos x1 -> x0, other arithmetic: 17 us -> none  [lon_tables(): return jnp.stack([jnp.cos(angles), -jnp.sin(angles)])]
  transfers between devices with their start and end apart: 3 -> 0, of which waited for: 3 -> 0; matrix products, arithmetic and copies ran while one was open for 6% -> 0% of each run, Pallas kernels for 0% -> 0%
where the time goes in v1:
time: 83.4 us; the launch traced here: 83.1 us
  Pallas kernels  76.8 us (92%)
  local copies, waits for them, and re-layouts  4.9 us (6%)
    pallas_call x1, Pallas kernels, on_device(): pl.pallas_call(kernel, out_shape=(jax.ShapeDtypeStruct((4, 5, 2, NN), F32...  76.8 us
    unnamed x10, local copies, waits for them, and re-layouts  4.77 us

profile of v1, /device:TPU:1, one launch (start us, length us, event | category | flops | bytes accessed | tf_op | source)
XLA Modules:
  0.0 83.1 jit_solution(16792294763011130028)
XLA Ops:
  0.6 0.7 convert_element_type.5
  1.3 0.0 copy-start.3
  1.3 0.1 convert_element_type.6.waves_ref
  1.5 0.6 copy-done.3
  2.0 0.0 copy-start
  2.0 1.1 %copy-done = f32[4,64,640]{2,1,0:T(8,128)S(1)} copy-done((f32[4,64,640]{2,1,0:T(8,128)S(1)}, f32[4,64,640]{2,1,0:T(8,128)}, u32[]{:S(2)}) %copy-start) | copy-done | bytes 655384
  3.1 0.0 copy-start.1
  3.1 0.9 %copy-done.1 = f32[2,8,4,640]{3,2,1,0:T(4,128)S(1)} copy-done((f32[2,8,4,640]{3,2,1,0:T(4,128)S(1)}, f32[2,8,4,640]{3,2,1,0:T(4,128)}, u32[]{:S(2)}) %copy-start.1) | copy-done | bytes 163864
  4.0 0.0 copy-start.2
  4.0 0.9 %copy-done.2 = f32[4,5,2,640]{3,2,1,0:T(2,128)S(1)} copy-done((f32[4,5,2,640]{3,2,1,0:T(2,128)S(1)}, f32[4,5,2,640]{3,2,1,0:T(2,128)}, u32[]{:S(2)}) %copy-start.2) | copy-done | bytes 102424
  4.9 76.8 %shard_map.59 = (f32[4,5,2,640]{3,2,1,0:T(2,128)S(1)}, f32[4,8,1440]{2,1,0:T(8,128)S(1)}) custom-call(f32[4,5,2,640]{3,2,1,0:T(2,128)S(1)} %copy-done.2, f32[64,10]{1,0:T(8,128)S(1)} %convert_element_type.6.waves_ref, s32[640]{0:T(1024)S(1)} %copy-done.3, f32[4,64,640]{2,1,0:T(8,128)S(1)} %copy-done, f32[2,8,4,640]{3,2,1,0:T(4,128)S(1)} %copy-done.1), custom_call_target="tpu_custom_call" | custom-call | tf_op jit(solution)/shard_map/pallas_call | solution.py:307
  81.8 0.6 copy.8
  82.4 0.7 copy.9
Async XLA Ops:
  1.3 0.7 copy-start.3
  2.0 1.1 %copy-start = (f32[4,64,640]{2,1,0:T(8,128)S(1)}, f32[4,64,640]{2,1,0:T(8,128)}, u32[]{:S(2)}) copy-start(f32[4,64,640]{2,1,0:T(8,128)} %constant.4.clone.coarse_ref) | copy-start | bytes 1966084
  3.1 0.9 %copy-start.1 = (f32[2,8,4,640]{3,2,1,0:T(4,128)S(1)}, f32[2,8,4,640]{3,2,1,0:T(4,128)}, u32[]{:S(2)}) copy-start(f32[2,8,4,640]{3,2,1,0:T(4,128)} %constant.5.clone.fine_ref) | copy-start | bytes 491524
  4.0 0.9 %copy-start.2 = (f32[4,5,2,640]{3,2,1,0:T(2,128)S(1)}, f32[4,5,2,640]{3,2,1,0:T(2,128)}, u32[]{:S(2)}) copy-start(f32[4,5,2,640]{3,2,1,0:T(2,128)} %x_ref.1) | copy-start | bytes 307204

commit v2 on v1

--- a/solution.py
+++ b/solution.py
@@ -61,8 +61,9 @@
 
 
 def kernel(
-    x_ref, waves_ref, wave_scalars, coarse_ref, fine_ref,
+    x_in, waves_in, scalars_in, coarse_in, fine_in,
     new_ref, products_ref,
+    x_ref, waves_ref, wave_scalars, coarse_ref, fine_ref, load_sem,
     spec, part, part_in, mer_hi, mer_lo, weights_x, lon_hi, lon_lo, weights_p,
     send1, recv1, send2, recv2, send3, recv3, grid, grid_in, final,
     pair_send, pair_recv, all_send, all_recv, lev_send, lev_recv,
@@ -73,8 +74,18 @@
     partner = {"lev": lax.rem(level + 2, 4)}
 
     def peer(step):
-        return lax.rem(chip + step, CHIPS)
-
+        turn = (step - 1) // 4
+        along_z = jnp.where(turn % 2 == 0, 8 + turn // 2, 8 - (turn + 1) // 2)
+        along_x = 3 - (step - 1) % 4
+        return lax.rem(chip // 16 + along_x, 4) * 16 + lax.rem(chip % 16 + along_z, 16)
+
+    loads = [
+        pltpu.make_async_copy(source, target, load_sem.at[index])
+        for index, (source, target) in enumerate((
+            (x_in, x_ref), (scalars_in, wave_scalars), (coarse_in, coarse_ref), (fine_in.at[core], fine_ref),
+            (waves_in, waves_ref)))]
+    for load in loads:
+        load.start()
     barrier = pltpu.get_barrier_semaphore()
 
     @pl.loop(1, CHIPS)
@@ -84,13 +95,17 @@
     pl.semaphore_signal(barrier, inc=1, device_id=sibling, device_id_type=MESH)
     pl.semaphore_signal(barrier, inc=1, device_id=partner, device_id_type=MESH)
 
+    loads[0].wait()
+    loads[1].wait()
     for s in range(5):
         for c in range(2):
             spec[5 * core + s, 4 * c:4 * c + 4, :] = x_ref[:, s, c, :]
 
+    loads[2].wait()
+    loads[3].wait()
     @pl.loop(0, 8)
     def _(row):
-        fine = fine_ref[core, row]
+        fine = fine_ref[row]
         for parity in range(2):
             fc, fs = fine[2 * parity:2 * parity + 1], fine[2 * parity + 1:2 * parity + 2]
             for block in range(4):
@@ -103,12 +118,13 @@
                 mer_hi[where, columns] = high
                 mer_lo[where, columns] = low
 
+    loads[4].wait()
     lane = lax.broadcasted_iota(jnp.int32, (16, 128), 1)
     lane_f = lane.astype(F32)
     for s in range(SLOTS):
         @pl.loop(0, 4)
         def _(block):
-            wave = waves_ref[pl.ds(pl.multiple_of(16 * block, 16), 16), s:s + 1] + jnp.zeros((16, 128), F32)
+            wave = waves_ref[pl.ds(pl.multiple_of(16 * block, 16), 16), s:s + 1].astype(F32) + jnp.zeros((16, 128), F32)
             cos, sin = cos_sin(wave * lane_f)
             turn_cos, turn_sin = cos_sin(wave * 128.0)
             first = pl.multiple_of(s * CHIPS + 16 * block, 16)
@@ -302,7 +318,7 @@
 
 def on_device(spectrum, wave_slot):
     coarse, fine = meridional_parts()
-    vmem, smem = pl.BlockSpec(memory_space=pltpu.VMEM), pl.BlockSpec(memory_space=pltpu.SMEM)
+    vmem, anywhere = pl.BlockSpec(memory_space=pltpu.VMEM), pl.BlockSpec(memory_space=pl.ANY)
     message = pltpu.VMEM((CHIPS, 5, 128), F32)
     return pl.pallas_call(
         kernel,
@@ -310,9 +326,15 @@
             jax.ShapeDtypeStruct((4, 5, 2, NN), F32),
             jax.ShapeDtypeStruct((4, 8, NLON), F32),
         ),
-        in_specs=[vmem, vmem, smem, vmem, vmem],
+        in_specs=[anywhere] * 5,
         out_specs=(vmem, vmem),
         scratch_shapes=[
+            pltpu.VMEM((4, 5, 2, NN), F32),
+            pltpu.VMEM((CHIPS, SLOTS), jnp.int32),
+            pltpu.SMEM((NN,), jnp.int32),
+            pltpu.VMEM((4, CHIPS, NN), F32),
+            pltpu.VMEM((8, 4, NN), F32),
+            pltpu.SemaphoreType.DMA((5,)),
             pltpu.VMEM((SLOTS, 8, NN), F32),
             pltpu.VMEM((SLOTS, 8, NN), F32),
             pltpu.VMEM((SLOTS, 8, NN), F32),
@@ -333,8 +355,8 @@
             pltpu.SemaphoreType.DMA((3,)),
             pltpu.SemaphoreType.DMA((3,)),
         ],
-        compiler_params=pltpu.CompilerParams(collective_id=0, has_side_effects=True, vmem_limit_bytes=48 << 20),
-    )(spectrum, wave_slot.reshape(CHIPS, SLOTS).astype(F32), wave_slot, jnp.asarray(coarse), jnp.asarray(fine))
+        compiler_params=pltpu.CompilerParams(collective_id=0, has_side_effects=True, vmem_limit_bytes=62 << 20),
+    )(spectrum, wave_slot.reshape(CHIPS, SLOTS), wave_slot, jnp.asarray(coarse), jnp.asarray(fine))
 
 
 def solution(mesh):

time: 83.4 us -> 75.8 us (0.909)
  Pallas kernels: 76.8 us -> 71.2 us
  local copies, waits for them, and re-layouts: 4.9 us -> 3.71 us
    pallas_call x1, Pallas kernels: 76.8 us -> 71.2 us  [on_device(): pl.pallas_call(kernel, out_shape=(jax.ShapeDtypeStruct((4, 5, 2, NN), F32...]
    unnamed x10 -> x4, local copies, waits for them, and re-layouts: 4.77 us -> 2.27 us
    reshape x0 -> x1, local copies, waits for them, and re-layouts: none -> 1.44 us  [on_device(): wave_slot.reshape(CHIPS, SLOTS)]
where the time goes in v2:
time: 75.8 us; the launch traced here: 75.6 us
  Pallas kernels  71.2 us (94%)
  local copies, waits for them, and re-layouts  3.71 us (5%)
    pallas_call x1, Pallas kernels, on_device(): pl.pallas_call(kernel, out_shape=(jax.ShapeDtypeStruct((4, 5, 2, NN), F32...  71.2 us
    unnamed x4, local copies, waits for them, and re-layouts  2.27 us

profile of v2, /device:TPU:1, one launch (start us, length us, event | category | flops | bytes accessed | tf_op | source)
XLA Modules:
  0.0 75.6 jit_solution(8787009007780071417)
XLA Ops:
  0.6 1.4 %reshape.7.waves_in = s32[64,10]{1,0:T(8,128)} reshape(s32[640]{0:T(1024)} %scalars_in.1) | data formatting | bytes 5120 | tf_op jit(solution)/shard_map/reshape | solution.py:359
  2.1 71.2 %shard_map.59 = (f32[4,5,2,640]{3,2,1,0:T(2,128)}, f32[4,8,1440]{2,1,0:T(8,128)}) custom-call(f32[4,5,2,640]{3,2,1,0:T(2,128)} %x_in.1, s32[64,10]{1,0:T(8,128)} %reshape.7.waves_in, s32[640]{0:T(1024)} %scalars_in.1, f32[4,64,640]{2,1,0:T(8,128)} %constant.4.clone.coarse_in, f32[2,8,4,640]{3,2,1,0:T(4,128)} %constant.5.clone.fine_in), custom_call_target="tpu_custom_call" | custom-call | tf_op jit(solution)/shard_map/pallas_call | solution.py:323
  73.3 0.0 copy-start
  73.3 1.6 %copy.8 = f32[4,5,2,640]{3,2,1,0:T(2,128)} copy(f32[4,5,2,640]{3,2,1,0:T(2,128)} %get-tuple-element.4) | data formatting | bytes 204800
  74.9 0.0 copy-done
  74.9 0.7 copy.9
Async XLA Ops:
  73.3 1.6 %copy-start = (f32[4,8,1440]{2,1,0:T(8,128)S(1)}, f32[4,8,1440]{2,1,0:T(8,128)}, u32[]{:S(2)}) copy-start(f32[4,8,1440]{2,1,0:T(8,128)} %get-tuple-element.5) | copy-start | bytes 552964

commit v3 on v2

--- a/solution.py
+++ b/solution.py
@@ -73,11 +73,23 @@
     sibling = {"grp": 2 * chip + 1 - core}
     partner = {"lev": lax.rem(level + 2, 4)}
 
-    def peer(step):
-        turn = (step - 1) // 4
-        along_z = jnp.where(turn % 2 == 0, 8 + turn // 2, 8 - (turn + 1) // 2)
-        along_x = 3 - (step - 1) % 4
-        return lax.rem(chip // 16 + along_x, 4) * 16 + lax.rem(chip % 16 + along_z, 16)
+    chip_z = lax.rem(chip, 16)
+    chip_rows = [16 * lax.rem(chip // 16 + along_x, 4) for along_x in range(4)]
+
+    def each_peer(act):
+        def plane(along_z, first_x):
+            z = lax.rem(chip_z + along_z, 16)
+            for along_x in range(3, first_x - 1, -1):
+                act(chip_rows[along_x] + z)
+
+        plane(8, 0)
+
+        @pl.loop(1, 8)
+        def _(turn):
+            plane(8 - turn, 0)
+            plane(8 + turn, 0)
+
+        plane(0, 1)
 
     loads = [
         pltpu.make_async_copy(source, target, load_sem.at[index])
@@ -88,10 +100,7 @@
         load.start()
     barrier = pltpu.get_barrier_semaphore()
 
-    @pl.loop(1, CHIPS)
-    def _(step):
-        pl.semaphore_signal(barrier, inc=1, device_id={"grp": 2 * peer(step) + core}, device_id_type=MESH)
-
+    each_peer(lambda to: pl.semaphore_signal(barrier, inc=1, device_id={"grp": 2 * to + core}, device_id_type=MESH))
     pl.semaphore_signal(barrier, inc=1, device_id=sibling, device_id_type=MESH)
     pl.semaphore_signal(barrier, inc=1, device_id=partner, device_id_type=MESH)
 
@@ -163,25 +172,31 @@
     def slot_wave(s):
         return wave_scalars[SLOTS * chip + s]
 
-    def exchange(index, out, inbox):
-        @pl.loop(1, CHIPS)
-        def _(step):
-            to = peer(step)
+    def start(index, half, out, inbox):
+        slot = 2 * index + half
+
+        def send(to):
             pltpu.make_async_remote_copy(
-                src_ref=out.at[to], dst_ref=inbox.at[chip], send_sem=all_send.at[index], recv_sem=all_recv.at[index],
+                src_ref=out.at[half, to], dst_ref=inbox.at[half, chip],
+                send_sem=all_send.at[slot], recv_sem=all_recv.at[slot],
                 device_id={"grp": 2 * to + core}, device_id_type=MESH).start()
 
-        inbox[chip] = out[chip]
-        arrived = inbox.at[pl.ds(0, CHIPS - 1)]
-        pltpu.make_async_copy(arrived, arrived, all_recv.at[index]).wait()
-        left = out.at[pl.ds(0, CHIPS - 1)]
-        pltpu.make_async_copy(left, left, all_send.at[index]).wait()
-
-    def meridional_synth(source, out):
+        each_peer(send)
+
+        inbox[half, chip] = out[half, chip]
+
+    def arrive(index, half, out, inbox):
+        slot = 2 * index + half
+        arrived = inbox.at[half, pl.ds(0, CHIPS - 1)]
+        pltpu.make_async_copy(arrived, arrived, all_recv.at[slot]).wait()
+        left = out.at[half, pl.ds(0, CHIPS - 1)]
+        pltpu.make_async_copy(left, left, all_send.at[slot]).wait()
+
+    def meridional_synth(index, source, out, inbox):
         for parity in range(2):
-            for half in range(5):
+            for two in range(5):
                 rows = []
-                for s in (2 * half, 2 * half + 1):
+                for s in (2 * two, 2 * two + 1):
                     wave = slot_wave(s)
                     odd = wave % 2
                     chosen = odd if parity else 1 - odd
@@ -189,48 +204,51 @@
                     rows.append(jnp.where(degree >= wave, source[s] * scale, 0.0))
                 high, low = split(jnp.concatenate(rows, axis=0))
                 columns = slice(NN * parity, NN * parity + NN)
-                weights_x[16 * half:16 * half + 16, columns] = high
-                weights_x[128 + 16 * half:128 + 16 * half + 16, columns] = low
-        both = dot_nt(mer_hi[...], weights_x[...])
-        value = both[:, :128] + both[:, 128:] + dot_nt(mer_lo[...], weights_x[:128, :])
-        tiles = [None] * 5
-
-        def put(t, piece):
-            tiles[t] = piece if tiles[t] is None else tiles[t] + piece
-
-        for row in range(8):
-            t, offset = divmod(80 * row, 128)
-            piece = value[CHIPS * row:CHIPS * row + CHIPS, :]
-            if offset:
-                piece = pltpu.roll(piece, offset, 1)
-            if offset + 80 > 128:
-                put(t, jnp.where(lane64 >= offset, piece, 0.0))
-                put(t + 1, jnp.where(lane64 < offset, piece, 0.0))
-            else:
-                put(t, piece)
-        for t in range(5):
-            out[:, t, :] = tiles[t]
-
-    def turned(inbox):
+                weights_x[16 * two:16 * two + 16, columns] = high
+                weights_x[128 + 16 * two:128 + 16 * two + 16, columns] = low
+        for half in range(2):
+            part_rows = slice(256 * half, 256 * half + 256)
+            both = dot_nt(mer_hi[part_rows, :], weights_x[...])
+            value = both[:, :128] + both[:, 128:] + dot_nt(mer_lo[part_rows, :], weights_x[:128, :])
+            tiles = [None] * 3
+
+            def put(t, piece):
+                tiles[t] = piece if tiles[t] is None else tiles[t] + piece
+
+            for row in range(4):
+                t, offset = divmod(80 * row, 128)
+                piece = value[CHIPS * row:CHIPS * row + CHIPS, :]
+                if offset:
+                    piece = pltpu.roll(piece, offset, 1)
+                if offset + 80 > 128:
+                    put(t, jnp.where(lane64 >= offset, piece, 0.0))
+                    put(t + 1, jnp.where(lane64 < offset, piece, 0.0))
+                else:
+                    put(t, piece)
+            for t in range(3):
+                out[half, :, t, :] = tiles[t]
+            start(index, half, out, inbox)
+
+    def turned(inbox, half):
         result = []
-        for t in range(5):
-            block = inbox[:, t, :]
+        for t in range(3):
+            block = inbox[half, :, t, :]
             result.append(jnp.concatenate([block, block], axis=0).T)
         return result
 
-    def longitude_operand(inbox):
-        tiles = turned(inbox)
+    def longitude_operand(inbox, half):
+        tiles = turned(inbox, half)
 
         def group(row, s):
             t, offset = divmod(80 * row + 8 * s, 128)
             return tiles[t][offset:offset + 8, :]
 
         real, imag = [], []
-        for pair in range(4):
+        for pair in range(2):
             real_row, imag_row = [], []
-            for half in range(5):
+            for two in range(5):
                 a, b = (
-                    jnp.where(lane8 < 64, group(row, 2 * half), group(row, 2 * half + 1))
+                    jnp.where(lane8 < 64, group(row, 2 * two), group(row, 2 * two + 1))
                     for row in (2 * pair, 2 * pair + 1))
                 real_row.append(jnp.where(sub8 < 4, a, pltpu.roll(b, 4, 0)))
                 imag_row.append(jnp.where(sub8 < 4, pltpu.roll(a, 4, 0), b))
@@ -241,54 +259,63 @@
 
     def longitude_synth(high, low, columns):
         both = dot_nn(jnp.concatenate([high, low], axis=0), lon_hi[:, columns])
-        return both[:32] + both[32:] + dot_nn(high, lon_lo[:, columns])
-
-    meridional_synth(spec, send1)
-    exchange(0, send1, recv1)
-    high, low = longitude_operand(recv1)
+        return both[:16] + both[16:] + dot_nn(high, lon_lo[:, columns])
+
+    meridional_synth(0, spec, send1, recv1)
     copies = []
-    for a in range(3):
-        grid[a] = longitude_synth(high, low, slice(512 * a, 512 * a + 512))
-        copy = pltpu.make_async_remote_copy(
-            src_ref=grid.at[a], dst_ref=grid_in.at[a], send_sem=lev_send.at[a], recv_sem=lev_recv.at[a],
-            device_id=partner, device_id_type=MESH)
-        copy.start()
-        copies.append(copy)
-    for a in range(3):
-        copies[a].wait()
-        here = grid[a]
-        high, low = split(here * grid_in[a] + here)
-        weights_p[0:32, 512 * a:512 * a + 512] = high
-        weights_p[128:160, 512 * a:512 * a + 512] = low
-
-    both = dot_nt(lon_hi[...], weights_p[...])
-    value = both[:, :128] + both[:, 128:] + dot_nt(lon_lo[...], weights_p[:128, :])
-    for t in range(5):
-        tile = None
-        for s in range(2):
-            for c in range(2):
-                first = (c * SLOTS + 2 * t + s) * CHIPS
-                piece = value[first:first + CHIPS, :]
-                offset = 64 * s + 32 * c
-                piece = pltpu.roll(piece, offset, 1) if offset else piece
-                tile = piece if tile is None else tile + piece
-        send2[:, t, :] = tile
-    exchange(1, send2, recv2)
-
-    tiles = turned(recv2)
-    rows = []
-    for s in range(SLOTS):
-        row = []
-        for pair in range(4):
-            a, b = (
-                tiles[s // 2][64 * (s % 2) + 32 * c + 8 * pair:64 * (s % 2) + 32 * c + 8 * pair + 8, :] for c in range(2))
-            left = jnp.where(sub8 < 4, a, pltpu.roll(b, 4, 0))
-            right = jnp.where(sub8 < 4, pltpu.roll(a, 4, 0), b)
-            row.append(jnp.where(lane8 < 64, left, right))
-        rows.append(jnp.concatenate(row, axis=1))
-    high, low = split(jnp.concatenate(rows, axis=0))
-    both = dot_nn(jnp.concatenate([high, low], axis=0), mer_hi[...])
-    value = both[:80] + both[80:] + dot_nn(high, mer_lo[...])
+    for half in range(2):
+        arrive(0, half, send1, recv1)
+        high, low = longitude_operand(recv1, half)
+        for a in range(3):
+            slot = 3 * half + a
+            grid[slot] = longitude_synth(high, low, slice(512 * a, 512 * a + 512))
+            copy = pltpu.make_async_remote_copy(
+                src_ref=grid.at[slot], dst_ref=grid_in.at[slot], send_sem=lev_send.at[slot], recv_sem=lev_recv.at[slot],
+                device_id=partner, device_id_type=MESH)
+            copy.start()
+            copies.append(copy)
+
+    for half in range(2):
+        for a in range(3):
+            slot = 3 * half + a
+            copies[slot].wait()
+            here = grid[slot]
+            high, low = split(here * grid_in[slot] + here)
+            weights_p[0:16, 512 * a:512 * a + 512] = high
+            weights_p[128:144, 512 * a:512 * a + 512] = low
+        both = dot_nt(lon_hi[...], weights_p[...])
+        value = both[:, :128] + both[:, 128:] + dot_nt(lon_lo[...], weights_p[:128, :])
+        for t in range(3):
+            tile = None
+            for s in range(4 * t, min(4 * t + 4, SLOTS)):
+                for c in range(2):
+                    first = (c * SLOTS + s) * CHIPS
+                    piece = value[first:first + CHIPS, :]
+                    offset = 32 * (s % 4) + 16 * c
+                    piece = pltpu.roll(piece, offset, 1) if offset else piece
+                    tile = piece if tile is None else tile + piece
+            send2[half, :, t, :] = tile
+        start(1, half, send2, recv2)
+
+    value = None
+    for half in range(2):
+        arrive(1, half, send2, recv2)
+        tiles = turned(recv2, half)
+        rows = []
+        for s in range(SLOTS):
+            row = []
+            for pair in range(2):
+                first = 32 * (s % 4) + 8 * pair
+                a, b = tiles[s // 4][first:first + 8, :], tiles[s // 4][first + 16:first + 24, :]
+                left = jnp.where(sub8 < 4, a, pltpu.roll(b, 4, 0))
+                right = jnp.where(sub8 < 4, pltpu.roll(a, 4, 0), b)
+                row.append(jnp.where(lane8 < 64, left, right))
+            rows.append(jnp.concatenate(row, axis=1))
+        high, low = split(jnp.concatenate(rows, axis=0))
+        part_rows = slice(256 * half, 256 * half + 256)
+        both = dot_nn(jnp.concatenate([high, low], axis=0), mer_hi[part_rows, :])
+        term = both[:80] + both[80:] + dot_nn(high, mer_lo[part_rows, :])
+        value = term if value is None else value + term
     for s in range(SLOTS):
         wave = slot_wave(s)
         odd = (wave % 2).astype(F32)
@@ -303,23 +330,25 @@
         for c in range(2):
             new_ref[:, s, c, :] = spec[5 * core + s, 4 * c:4 * c + 4, :]
 
-    meridional_synth(spec, send3)
-    exchange(2, send3, recv3)
-    high, low = longitude_operand(recv3)
-    for a in range(3):
-        value = longitude_synth(high, low, slice(512 * a, 512 * a + 512))
-        for b in range(4):
-            tile = 4 * a + b
-            width = min(128, NLON - 128 * tile)
-            final[tile] = value[:, 128 * b:128 * b + 128]
-            for l in range(4):
-                products_ref[l, :, 128 * tile:128 * tile + width] = final[tile, pl.ds(l, 8, stride=4), :][:, :width]
+    meridional_synth(2, spec, send3, recv3)
+    for half in range(2):
+        arrive(2, half, send3, recv3)
+        high, low = longitude_operand(recv3, half)
+        for a in range(3):
+            value = longitude_synth(high, low, slice(512 * a, 512 * a + 512))
+            for b in range(4):
+                tile = 4 * a + b
+                width = min(128, NLON - 128 * tile)
+                final[tile, 16 * half:16 * half + 16, :] = value[:, 128 * b:128 * b + 128]
+                if half:
+                    for l in range(4):
+                        products_ref[l, :, 128 * tile:128 * tile + width] = final[tile, pl.ds(l, 8, stride=4), :][:, :width]
 
 
 def on_device(spectrum, wave_slot):
     coarse, fine = meridional_parts()
     vmem, anywhere = pl.BlockSpec(memory_space=pltpu.VMEM), pl.BlockSpec(memory_space=pl.ANY)
-    message = pltpu.VMEM((CHIPS, 5, 128), F32)
+    message = pltpu.VMEM((2, CHIPS, 3, 128), F32)
     return pl.pallas_call(
         kernel,
         out_shape=(
@@ -345,15 +374,15 @@
             pltpu.VMEM((2 * SLOTS * CHIPS, LANES), BF16),
             pltpu.VMEM((256, LANES), BF16),
             message, message, message, message, message, message,
-            pltpu.VMEM((3, 32, 512), F32),
-            pltpu.VMEM((3, 32, 512), F32),
+            pltpu.VMEM((6, 16, 512), F32),
+            pltpu.VMEM((6, 16, 512), F32),
             pltpu.VMEM((12, 32, 128), F32),
             pltpu.SemaphoreType.DMA((2,)),
             pltpu.SemaphoreType.DMA((2,)),
-            pltpu.SemaphoreType.DMA((3,)),
-            pltpu.SemaphoreType.DMA((3,)),
-            pltpu.SemaphoreType.DMA((3,)),
-            pltpu.SemaphoreType.DMA((3,)),
+            pltpu.SemaphoreType.DMA((6,)),
+            pltpu.SemaphoreType.DMA((6,)),
+            pltpu.SemaphoreType.DMA((6,)),
+            pltpu.SemaphoreType.DMA((6,)),
         ],
         compiler_params=pltpu.CompilerParams(collective_id=0, has_side_effects=True, vmem_limit_bytes=62 << 20),
     )(spectrum, wave_slot.reshape(CHIPS, SLOTS), wave_slot, jnp.asarray(coarse), jnp.asarray(fine))

time: 75.8 us -> 73.3 us (0.967)
  Pallas kernels: 71.2 us -> 68.8 us
    pallas_call x1, Pallas kernels: 71.2 us -> 68.8 us  [on_device(): pl.pallas_call(kernel, out_shape=(jax.ShapeDtypeStruct((4, 5, 2, NN), F32...]
where the time goes in v3:
time: 73.3 us; the launch traced here: 73.1 us
  Pallas kernels  68.8 us (94%)
  local copies, waits for them, and re-layouts  3.71 us (5%)
    pallas_call x1, Pallas kernels, on_device(): pl.pallas_call(kernel, out_shape=(jax.ShapeDtypeStruct((4, 5, 2, NN), F32...  68.8 us
    unnamed x4, local copies, waits for them, and re-layouts  2.27 us

profile of v3, /device:TPU:1, one launch (start us, length us, event | category | flops | bytes accessed | tf_op | source)
XLA Modules:
  0.0 73.1 jit_solution(17802712932736568101)
XLA Ops:
  0.6 1.4 %reshape.7.waves_in = s32[64,10]{1,0:T(8,128)} reshape(s32[640]{0:T(1024)} %scalars_in.1) | data formatting | bytes 5120 | tf_op jit(solution)/shard_map/reshape | solution.py:388
  2.1 68.8 %shard_map.59 = (f32[4,5,2,640]{3,2,1,0:T(2,128)}, f32[4,8,1440]{2,1,0:T(8,128)}) custom-call(f32[4,5,2,640]{3,2,1,0:T(2,128)} %x_in.1, s32[64,10]{1,0:T(8,128)} %reshape.7.waves_in, s32[640]{0:T(1024)} %scalars_in.1, f32[4,64,640]{2,1,0:T(8,128)} %constant.4.clone.coarse_in, f32[2,8,4,640]{3,2,1,0:T(4,128)} %constant.5.clone.fine_in), custom_call_target="tpu_custom_call" | custom-call | tf_op jit(solution)/shard_map/pallas_call | solution.py:352
  70.8 0.0 copy-start
  70.8 1.6 %copy.8 = f32[4,5,2,640]{3,2,1,0:T(2,128)} copy(f32[4,5,2,640]{3,2,1,0:T(2,128)} %get-tuple-element.4) | data formatting | bytes 204800
  72.4 0.0 copy-done
  72.4 0.7 copy.9
Async XLA Ops:
  70.8 1.6 %copy-start = (f32[4,8,1440]{2,1,0:T(8,128)S(1)}, f32[4,8,1440]{2,1,0:T(8,128)}, u32[]{:S(2)}) copy-start(f32[4,8,1440]{2,1,0:T(8,128)} %get-tuple-element.5) | copy-start | bytes 552964
